TPU v7x, 32 devices: a whole 2x2x4 slice. The times are simulated.
32 devices in a mesh: leaf: 8 (over z, y), fsdp: 4 (over x, core).
Axes of the slice: x: 2, y: 2, z: 4, core: 2. Of those that a mesh axis runs over, the one named last changes fastest.
Arguments:
- hidden: bfloat16 [4, 2048, 768], P('fsdp', 'leaf'), may hold values from -6 to 6
- noise_mask: int32 [4, 2048], P('fsdp', 'leaf'), may hold values 0 or 1
- seg_blocks: int32 [4, 128], P('fsdp'), may hold values from 0 to 12, as said below
- parents: int32 [4, 13], P('fsdp'), may hold values from 0 to 4, as said below
- ln1_gain: bfloat16 [768], P(('leaf', 'fsdp')), may hold values from 0.099609375 to 1.8984375
- w_qkv: bfloat16 [768, 2304], P(('leaf', 'fsdp')), may hold values from -0.21875 to 0.21875
- w_out: bfloat16 [768, 768], P(('leaf', 'fsdp')), may hold values from -3.5 to 3.5
- ln2_gain: bfloat16 [768], P(('leaf', 'fsdp')), may hold values from 0.099609375 to 1.8984375
- w_up: bfloat16 [768, 3072], P(('leaf', 'fsdp')), may hold values from -0.21875 to 0.21875
- up_bias: bfloat16 [3072], P(('leaf', 'fsdp')), may hold values from -3 to 3
- w_down: bfloat16 [3072, 768], P(('leaf', 'fsdp')), may hold values from -0.109375 to 0.109375
- down_bias: bfloat16 [768], P(('leaf', 'fsdp')), may hold values from -2 to 2
- mask_embed: bfloat16 [768], P(('leaf', 'fsdp')), may hold values from -5 to 5
- cotangent: bfloat16 [4, 2, 2048, 768], P('fsdp', None, 'leaf'), may hold values from -6 to 6
Outputs:
- output: bfloat16 [4, 2, 2048, 768], P('fsdp', None, 'leaf')
- grad_hidden: bfloat16 [4, 2048, 768], P('fsdp', 'leaf')
- grad_ln1_gain: float32 [768], P(('leaf', 'fsdp'))
- grad_w_qkv: float32 [768, 2304], P(('leaf', 'fsdp'))
- grad_w_out: float32 [768, 768], P(('leaf', 'fsdp'))
- grad_ln2_gain: float32 [768], P(('leaf', 'fsdp'))
- grad_w_up: float32 [768, 3072], P(('leaf', 'fsdp'))
- grad_up_bias: float32 [3072], P(('leaf', 'fsdp'))
- grad_w_down: float32 [3072, 768], P(('leaf', 'fsdp'))
- grad_down_bias: float32 [768], P(('leaf', 'fsdp'))
- grad_mask_embed: float32 [768], P(('leaf', 'fsdp'))
Inputs may be any that keep to these rules, and one draw needn't show every extreme that they name: `seg_blocks`: segment numbers never fall along a tree; segment 0 holds the first 64 blocks (rounded down); every other segment has one block or more; the last segment ends the tree. `parents`: segment 0 is the trunk with parent 0; segments 1 to 4 have parent 0; each of them is the parent of exactly 2 of the segments above 4.
All inputs are finite; a program needn't handle non-finite values. No bound on the sum of `noise_mask` on one device may be relied on, other than what follows from the above.
Results may differ from a plain program's by a relative error of at most 0.015.
Values may be sent and summed in bfloat16 or wider, within the bound.
No kernel may reach another device: no remote copies, remote signals or barrier semaphores. Data moves between devices by JAX's collectives and lax.ppermute only.
A program may use at most 256 MiB of HBM per device.

v0:
```python
import math
import jax
import jax.numpy as jnp
from jax import lax
from jax.sharding import PartitionSpec as P

HEAD_DIM = 64
BLOCK = 16
NEG_FILL = -1000000000.0
EPSILON = 1e-05


def look_up(table, indices):
    slots = jnp.arange(table.shape[0], dtype=jnp.int32)
    hits = indices[..., None] == slots
    return jnp.sum(jnp.where(hits, table, 0), axis=-1)


def tree_layout(seg_row, parent_row):
    slots = jnp.arange(parent_row.shape[0], dtype=jnp.int32)
    seg_lengths = jnp.sum((seg_row[:, None] == slots).astype(jnp.int32), axis=0)
    seg_starts = jnp.cumsum(seg_lengths) - seg_lengths
    grand_parent = look_up(parent_row, parent_row)
    offsets = jnp.where(slots > 0, look_up(seg_lengths, parent_row), 0) + jnp.where(
        parent_row > 0, look_up(seg_lengths, grand_parent), 0
    )
    block_ids = jnp.arange(seg_row.shape[0], dtype=jnp.int32)
    path_block = look_up(offsets, seg_row) + block_ids - look_up(seg_starts, seg_row)
    return (path_block, look_up(parent_row, seg_row), look_up(grand_parent, seg_row))


def layer_norm(values, gain):
    centred = values - jnp.mean(values, axis=-1, keepdims=True)
    spread = jnp.mean(centred * centred, axis=-1, keepdims=True)
    return centred * lax.rsqrt(spread + EPSILON) * gain


def gelu_tanh(values):
    return jax.nn.gelu(values, approximate=True)


def rotate(values, cosine, sine):
    half = values.shape[-1] // 2
    first = values[..., :half]
    second = values[..., half:]
    return jnp.concatenate(
        [first * cosine - second * sine, second * cosine + first * sine], axis=-1
    )


def to_heads(values, heads):
    return values.reshape(values.shape[0], heads, HEAD_DIM).transpose(1, 0, 2)


def from_heads(values):
    return values.transpose(1, 0, 2).reshape(values.shape[1], values.shape[0] * values.shape[2])


def shards(
    hidden,
    noise_mask,
    seg_blocks,
    parents,
    ln1_gain,
    w_qkv,
    w_out,
    ln2_gain,
    w_up,
    up_bias,
    w_down,
    down_bias,
    mask_embed,
    cotangent,
):
    gathered = (
        lax.all_gather(ln1_gain, ("leaf", "fsdp"), axis=0, tiled=True),
        lax.all_gather(w_qkv, ("leaf", "fsdp"), axis=0, tiled=True),
        lax.all_gather(w_out, ("leaf", "fsdp"), axis=0, tiled=True),
        lax.all_gather(ln2_gain, ("leaf", "fsdp"), axis=0, tiled=True),
        lax.all_gather(w_up, ("leaf", "fsdp"), axis=0, tiled=True),
        lax.all_gather(up_bias, ("leaf", "fsdp"), axis=0, tiled=True),
        lax.all_gather(w_down, ("leaf", "fsdp"), axis=0, tiled=True),
        lax.all_gather(down_bias, ("leaf", "fsdp"), axis=0, tiled=True),
        lax.all_gather(mask_embed, ("leaf", "fsdp"), axis=0, tiled=True),
    )
    gain_one, qkv_w, out_w, gain_two, up_w, up_b, down_w, down_b, embed = gathered
    rows_dev = hidden.shape[1]
    width = hidden.shape[2]
    heads = width // HEAD_DIM
    blocks_dev = rows_dev // BLOCK
    leaf_rank = lax.axis_index("leaf")
    seg_row = seg_blocks[0]
    path_block, first_up, second_up = tree_layout(seg_row, parents[0])
    first_block = leaf_rank * blocks_dev
    own_seg = lax.dynamic_slice_in_dim(seg_row, first_block, blocks_dev)
    own_path = lax.dynamic_slice_in_dim(path_block, first_block, blocks_dev)
    own_first = lax.dynamic_slice_in_dim(first_up, first_block, blocks_dev)
    own_second = lax.dynamic_slice_in_dim(second_up, first_block, blocks_dev)
    related = (
        (seg_row[None, :] == own_seg[:, None])
        | (seg_row[None, :] == own_first[:, None])
        | (seg_row[None, :] == own_second[:, None])
    )
    clean_ok = related & (path_block[None, :] <= own_path[:, None])
    noisy_ok = related & (path_block[None, :] < own_path[:, None])
    clean_tok = jnp.repeat(jnp.repeat(clean_ok, BLOCK, axis=0), BLOCK, axis=1)
    noisy_tok = jnp.repeat(jnp.repeat(noisy_ok, BLOCK, axis=0), BLOCK, axis=1)
    row_block = jnp.arange(rows_dev, dtype=jnp.int32) // BLOCK
    same_block = row_block[:, None] == row_block[None, :]
    mask_all = jnp.concatenate(
        [
            jnp.concatenate([clean_tok, jnp.zeros_like(same_block)], axis=1),
            jnp.concatenate([noisy_tok, same_block], axis=1),
        ],
        axis=0,
    )
    offsets_in = jnp.arange(BLOCK, dtype=jnp.int32)
    positions = (own_path[:, None] * BLOCK + offsets_in).reshape(rows_dev).astype(jnp.float32)
    positions = jnp.concatenate([positions, positions])
    freqs = jnp.exp(
        jnp.arange(HEAD_DIM // 2, dtype=jnp.float32) * (-math.log(10000.0) / (HEAD_DIM // 2))
    )
    angles = positions[:, None, None] * freqs
    cosine = jnp.cos(angles)
    sine = jnp.sin(angles)
    clean = hidden[0].astype(jnp.float32)
    masked = (noise_mask[0] == 1)[:, None]
    noisy = jnp.where(masked, embed.astype(jnp.float32)[None, :], clean)
    stream = jnp.concatenate([clean, noisy], axis=0)
    gain_one_f = gain_one.astype(jnp.float32)
    gain_two_f = gain_two.astype(jnp.float32)
    normed_one = layer_norm(stream, gain_one_f).astype(jnp.bfloat16)
    projected = jnp.dot(normed_one, qkv_w, preferred_element_type=jnp.float32)
    query = rotate(
        projected[:, :width].reshape(2 * rows_dev, heads, HEAD_DIM), cosine, sine
    ).reshape(2 * rows_dev, width)
    keyed = rotate(
        projected[:, width : 2 * width].reshape(2 * rows_dev, heads, HEAD_DIM), cosine, sine
    ).reshape(2 * rows_dev, width)
    query_low = query.astype(jnp.bfloat16)
    key_low = keyed.astype(jnp.bfloat16)
    value_low = projected[:, 2 * width :].astype(jnp.bfloat16)
    tree_keys, tree_values = (
        lax.all_gather(key_low[:rows_dev], "leaf", axis=0, tiled=True),
        lax.all_gather(value_low[:rows_dev], "leaf", axis=0, tiled=True),
    )
    tree_tok = tree_keys.shape[0]
    keys_all = jnp.concatenate([tree_keys, key_low[rows_dev:]], axis=0)
    values_all = jnp.concatenate([tree_values, value_low[rows_dev:]], axis=0)
    q_heads = to_heads(query_low, heads)

    def head_forward(operands):
        q_head, k_head, v_head = operands
        raw = jnp.einsum("qd,kd->qk", q_head, k_head, preferred_element_type=jnp.float32) * 0.125
        scores = jnp.where(mask_all, raw, NEG_FILL)
        top_score = jnp.max(scores, axis=-1, keepdims=True)
        expd = jnp.exp(scores - top_score)
        total = jnp.sum(expd, axis=-1, keepdims=True)
        probs = (expd / total).astype(jnp.bfloat16)
        return (
            jnp.dot(probs, v_head, preferred_element_type=jnp.float32),
            top_score + jnp.log(total),
        )

    attended, log_norm = lax.map(
        head_forward, (q_heads, to_heads(keys_all, heads), to_heads(values_all, heads))
    )
    mixed_low = from_heads(attended).astype(jnp.bfloat16)
    after = stream + jnp.dot(mixed_low, out_w, preferred_element_type=jnp.float32)
    normed_two = layer_norm(after, gain_two_f).astype(jnp.bfloat16)
    pre_act = jnp.dot(normed_two, up_w, preferred_element_type=jnp.float32) + up_b.astype(
        jnp.float32
    )
    activated = gelu_tanh(pre_act).astype(jnp.bfloat16)
    result = (
        after
        + jnp.dot(activated, down_w, preferred_element_type=jnp.float32)
        + down_b.astype(jnp.float32)
    )
    output = result.astype(jnp.bfloat16).reshape(1, 2, rows_dev, width)
    regathered = (
        lax.all_gather(ln1_gain, ("leaf", "fsdp"), axis=0, tiled=True),
        lax.all_gather(w_qkv, ("leaf", "fsdp"), axis=0, tiled=True),
        lax.all_gather(w_out, ("leaf", "fsdp"), axis=0, tiled=True),
        lax.all_gather(ln2_gain, ("leaf", "fsdp"), axis=0, tiled=True),
        lax.all_gather(w_up, ("leaf", "fsdp"), axis=0, tiled=True),
        lax.all_gather(up_bias, ("leaf", "fsdp"), axis=0, tiled=True),
        lax.all_gather(w_down, ("leaf", "fsdp"), axis=0, tiled=True),
        lax.all_gather(down_bias, ("leaf", "fsdp"), axis=0, tiled=True),
        lax.all_gather(mask_embed, ("leaf", "fsdp"), axis=0, tiled=True),
    )
    qkv_back, out_back, up_back, down_back = (
        regathered[1],
        regathered[2],
        regathered[4],
        regathered[6],
    )
    grad_out = cotangent[0].astype(jnp.float32).reshape(2 * rows_dev, width)
    grad_two = grad_out.astype(jnp.bfloat16)
    grad_down_b = jnp.sum(grad_two.astype(jnp.float32), axis=0)
    grad_down_w = jnp.einsum("rf,rd->fd", activated, grad_two, preferred_element_type=jnp.float32)
    grad_act = jnp.einsum("rd,fd->rf", grad_two, down_back, preferred_element_type=jnp.float32)
    gelu_out, gelu_back = jax.vjp(gelu_tanh, pre_act)
    grad_pre = gelu_back(grad_act)[0].astype(jnp.bfloat16)
    grad_up_b = jnp.sum(grad_pre.astype(jnp.float32), axis=0)
    grad_up_w = jnp.einsum("rd,rf->df", normed_two, grad_pre, preferred_element_type=jnp.float32)
    grad_normed_two = jnp.einsum("rf,df->rd", grad_pre, up_back, preferred_element_type=jnp.float32)
    norm_out, norm_back = jax.vjp(layer_norm, after, gain_two_f)
    grad_after_ln, grad_gain_two = norm_back(grad_normed_two)
    grad_after = grad_out + grad_after_ln
    grad_one = grad_after.astype(jnp.bfloat16)
    grad_out_w = jnp.einsum("rd,re->de", mixed_low, grad_one, preferred_element_type=jnp.float32)
    grad_mixed = jnp.einsum(
        "re,de->rd", grad_one, out_back, preferred_element_type=jnp.float32
    ).astype(jnp.bfloat16)
    back_keys, back_values = (
        lax.all_gather(key_low[:rows_dev], "leaf", axis=0, tiled=True),
        lax.all_gather(value_low[:rows_dev], "leaf", axis=0, tiled=True),
    )
    keys_back = jnp.concatenate([back_keys, key_low[rows_dev:]], axis=0)
    values_back = jnp.concatenate([back_values, value_low[rows_dev:]], axis=0)

    def head_backward(operands):
        q_head, k_head, v_head, g_head, norm_head = operands
        raw = jnp.einsum("qd,kd->qk", q_head, k_head, preferred_element_type=jnp.float32) * 0.125
        scores = jnp.where(mask_all, raw, NEG_FILL)
        probs = jnp.exp(scores - norm_head)
        grad_v = jnp.einsum(
            "qk,qd->kd", probs.astype(jnp.bfloat16), g_head, preferred_element_type=jnp.float32
        )
        grad_p = jnp.einsum("qd,kd->qk", g_head, v_head, preferred_element_type=jnp.float32)
        inner = jnp.sum(probs * grad_p, axis=-1, keepdims=True)
        grad_s = (probs * (grad_p - inner)).astype(jnp.bfloat16)
        grad_q = jnp.einsum("qk,kd->qd", grad_s, k_head, preferred_element_type=jnp.float32) * 0.125
        grad_k = jnp.einsum("qk,qd->kd", grad_s, q_head, preferred_element_type=jnp.float32) * 0.125
        return (grad_q, grad_k, grad_v)

    grad_q_heads, grad_k_heads, grad_v_heads = lax.map(
        head_backward,
        (
            q_heads,
            to_heads(keys_back, heads),
            to_heads(values_back, heads),
            to_heads(grad_mixed, heads),
            log_norm,
        ),
    )
    grad_query = from_heads(grad_q_heads)
    grad_keys_all = from_heads(grad_k_heads)
    grad_values_all = from_heads(grad_v_heads)
    own_key_grad, own_value_grad = (
        lax.psum_scatter(
            grad_keys_all[:tree_tok].astype(jnp.bfloat16), "leaf", scatter_dimension=0, tiled=True
        ).astype(jnp.float32),
        lax.psum_scatter(
            grad_values_all[:tree_tok].astype(jnp.bfloat16), "leaf", scatter_dimension=0, tiled=True
        ).astype(jnp.float32),
    )
    grad_key = jnp.concatenate([own_key_grad, grad_keys_all[tree_tok:]], axis=0)
    grad_value = jnp.concatenate([own_value_grad, grad_values_all[tree_tok:]], axis=0)
    grad_query = rotate(grad_query.reshape(2 * rows_dev, heads, HEAD_DIM), cosine, -sine).reshape(
        2 * rows_dev, width
    )
    grad_key = rotate(grad_key.reshape(2 * rows_dev, heads, HEAD_DIM), cosine, -sine).reshape(
        2 * rows_dev, width
    )
    grad_proj = jnp.concatenate([grad_query, grad_key, grad_value], axis=1).astype(jnp.bfloat16)
    grad_qkv_w = jnp.einsum("rd,re->de", normed_one, grad_proj, preferred_element_type=jnp.float32)
    grad_normed_one = jnp.einsum(
        "re,de->rd", grad_proj, qkv_back, preferred_element_type=jnp.float32
    )
    first_out, first_back = jax.vjp(layer_norm, stream, gain_one_f)
    grad_stream_ln, grad_gain_one = first_back(grad_normed_one)
    grad_stream = grad_after + grad_stream_ln
    grad_clean = grad_stream[:rows_dev] + jnp.where(masked, 0.0, grad_stream[rows_dev:])
    grad_embed = jnp.sum(jnp.where(masked, grad_stream[rows_dev:], 0.0), axis=0)
    summed = (
        lax.psum_scatter(grad_gain_one, ("leaf", "fsdp"), scatter_dimension=0, tiled=True),
        lax.psum_scatter(grad_qkv_w, ("leaf", "fsdp"), scatter_dimension=0, tiled=True),
        lax.psum_scatter(grad_out_w, ("leaf", "fsdp"), scatter_dimension=0, tiled=True),
        lax.psum_scatter(grad_gain_two, ("leaf", "fsdp"), scatter_dimension=0, tiled=True),
        lax.psum_scatter(grad_up_w, ("leaf", "fsdp"), scatter_dimension=0, tiled=True),
        lax.psum_scatter(grad_up_b, ("leaf", "fsdp"), scatter_dimension=0, tiled=True),
        lax.psum_scatter(grad_down_w, ("leaf", "fsdp"), scatter_dimension=0, tiled=True),
        lax.psum_scatter(grad_down_b, ("leaf", "fsdp"), scatter_dimension=0, tiled=True),
        lax.psum_scatter(grad_embed, ("leaf", "fsdp"), scatter_dimension=0, tiled=True),
    )
    return (
        output,
        grad_clean.astype(jnp.bfloat16)[None],
        summed[0],
        summed[1],
        summed[2],
        summed[3],
        summed[4],
        summed[5],
        summed[6],
        summed[7],
        summed[8],
    )


def solution(mesh):
    in_specs = (
        P("fsdp", "leaf", None),
        P("fsdp", "leaf"),
        P("fsdp", None),
        P("fsdp", None),
        P(("leaf", "fsdp")),
        P(("leaf", "fsdp"), None),
        P(("leaf", "fsdp"), None),
        P(("leaf", "fsdp")),
        P(("leaf", "fsdp"), None),
        P(("leaf", "fsdp")),
        P(("leaf", "fsdp"), None),
        P(("leaf", "fsdp")),
        P(("leaf", "fsdp")),
        P("fsdp", None, "leaf", None),
    )
    out_specs = (
        P("fsdp", None, "leaf", None),
        P("fsdp", "leaf", None),
        P(("leaf", "fsdp")),
        P(("leaf", "fsdp"), None),
        P(("leaf", "fsdp"), None),
        P(("leaf", "fsdp")),
        P(("leaf", "fsdp"), None),
        P(("leaf", "fsdp")),
        P(("leaf", "fsdp"), None),
        P(("leaf", "fsdp")),
        P(("leaf", "fsdp")),
    )
    return jax.shard_map(shards, mesh=mesh, in_specs=in_specs, out_specs=out_specs, check_vma=False)
```

profile of v0, /device:TPU:0, one launch (start us, length us, event | category | flops | bytes accessed | tf_op | source)
XLA Modules:
  0.0 1240.7 jit_solution(11994550310879820292)
XLA Ops:
  12.2 42.3 %all-reduce.12 = (bf16[768]{0:T(1024)(128)(2,1)S(1)}, bf16[768]{0:T(1024)(128)(2,1)S(1)}, bf16[768]{0:T(1024)(128)(2,1)}, bf16[768]{0:T(1024)(128)(2,1)S(1)}, bf16[3072]{0:T(1024)(128)(2,1)S(1)}) all-reduce(bf16[768]{0:T(1024)(128)(2,1)S(1)} %dynamic-update-slice.1, ...), channel_id=1, replica_groups=mesh['leaf'=8,'fsdp'=4] {'leaf','fsdp'}, use_global_device_ids=true, to_apply=%add.2 | all-reduce | flops 6144 | bytes 24576
  58.5 15.2 %all-gather.7.cloned.1.call-done = bf16[768,2304]{1,0:T(8,128)(2,1)} async-done(((bf16[24,2304]{1,0:T(8,128)(2,1)}), bf16[768,2304]{1,0:T(8,128)(2,1)}) %all-gather.7.cloned.1.call-update) | async-done | bytes 3538960 | tf_op jit(solution)/shard_map/all_gather | solution.py:77
  73.8 6.2 fusion.73
  105.6 34.7 %all-gather.11.cloned.1.call-done = bf16[2048,768]{1,0:T(8,128)(2,1)} async-done(((bf16[256,768]{1,0:T(8,128)(2,1)}), bf16[2048,768]{1,0:T(8,128)(2,1)}) %all-gather.11.cloned.1.call-update) | async-done | bytes 3145744 | tf_op jit(solution)/shard_map/all_gather | solution.py:145
  150.2 53.8 %all-gather.9.cloned.1.call-done = bf16[2048,768]{0,1:T(8,128)(2,1)} async-done(((bf16[256,768]{0,1:T(8,128)(2,1)}), bf16[2048,768]{0,1:T(8,128)(2,1)}) %all-gather.9.cloned.1.call-update) | async-done | bytes 3145744 | tf_op jit(solution)/shard_map/all_gather | solution.py:144
  208.1 7.9 copy.82
  216.0 8.0 copy.84
  224.0 69.5 %while.28 = (s32[]{:T(128)}, bf16[12,512,64]{1,2,0:T(8,128)(2,1)S(1)}, f32[12,512,1]{1,2,0:T(1,128)}, bf16[12,512,64]{2,1,0:T(8,128)(2,1)}, bf16[12,2304,64]{2,1...) while((s32[]{:T(128)}, ...), condition=%wide.region_14.15_spmd.clone, body=%wide.region_11.14_spmd.sunk.clone | while | flops 311426560 | bytes 16799832 | solution.py:165
  297.5 27.0 %all-gather.15.cloned.1.call-done = bf16[768,3072]{1,0:T(8,128)(2,1)} async-done(((bf16[24,3072]{1,0:T(8,128)(2,1)}), bf16[768,3072]{1,0:T(8,128)(2,1)}) %all-gather.15.cloned.1.call-update) | async-done | bytes 4718608 | tf_op jit(solution)/shard_map/all_gather | solution.py:80
  324.5 8.2 fusion.64
  332.7 57.0 %all-gather.17.cloned.1.call-done = bf16[3072,768]{1,0:T(8,128)(2,1)} async-done(((bf16[96,768]{1,0:T(8,128)(2,1)}), bf16[3072,768]{1,0:T(8,128)(2,1)}) %all-gather.17.cloned.1.call-update) | async-done | bytes 4718608 | tf_op jit(solution)/shard_map/all_gather | solution.py:82
  389.7 9.9 convert_reduce_fusion
  410.1 154.7 %while.29 = (s32[]{:T(128)}, f32[12,512,64]{1,2,0:T(8,128)}, f32[12,2304,64]{1,2,0:T(8,128)}, bf16[12,2304,64]{1,2,0:T(8,128)(2,1)}, bf16[12,512,64]{2,1,0:T(8,1...) while((s32[]{:T(128)}, f32[12,512,64]{1,2,0:T(8,128)}, ...), condition=%wide.region_21.22_spmd.clone, body=%wide.region_19.21_spmd.sunk.clone | while | flops 765771264 | bytes 40057968 | solution.py:238
  578.3 10.1 fusion.66
  589.9 7.2 fusion.63
  601.2 42.4 %reduce-scatter.7.cloned.1.call-done = bf16[256,768]{0,1:T(8,128)(2,1)} async-done(((bf16[2048,768]{0,1:T(8,128)(2,1)}), bf16[256,768]{0,1:T(8,128)(2,1)}) %reduce-scatter.7.cloned.1.call-update) | async-done | bytes 393232 | tf_op jit(solution)/shard_map/reduce_scatter | solution.py:252
  648.9 72.4 %reduce-scatter.9.cloned.1.call-done = bf16[256,768]{0,1:T(8,128)(2,1)} async-done(((bf16[2048,768]{0,1:T(8,128)(2,1)}), bf16[256,768]{0,1:T(8,128)(2,1)}) %reduce-scatter.9.cloned.1.call-update) | async-done | bytes 393232 | tf_op jit(solution)/shard_map/reduce_scatter | solution.py:255
  721.3 6.7 fusion.52
  730.6 9.3 add_convert_fusion
  745.6 40.2 %all-reduce.11 = (f32[768]{0:T(1024)S(1)}, f32[768]{0:T(1024)S(1)}, f32[3072]{0:T(1024)S(1)}, f32[768]{0:T(1024)S(1)}, f32[768]{0:T(1024)S(1)}) all-reduce(f32[768]{0:T(1024)S(1)} %get-tuple-element.195, f32[768]{0:T(1024)S(1)} %copy-done.34, f32[3072]{0:T(1024)S(1)} %copy-done.31, ...), channel_id=4, replica_groups=mesh['leaf'=8,'fsdp'=4] {'leaf','fsdp'}, use_global_device_ids=true, to_apply=%region_27.28.clone | all-reduce | flops 6144 | bytes 49152
  788.8 36.7 %reduce-scatter.13.cloned.1.call-done = f32[24,768]{1,0:T(8,128)} async-done(((f32[768,768]{1,0:T(8,128)}), f32[24,768]{1,0:T(8,128)}) %reduce-scatter.13.cloned.1.call-update) | async-done | bytes 73744 | tf_op jit(solution)/shard_map/reduce_scatter | solution.py:280
  825.5 141.8 %reduce-scatter.17.cloned.1.call-done = f32[96,768]{1,0:T(8,128)} async-done(((f32[3072,768]{1,0:T(8,128)}), f32[96,768]{1,0:T(8,128)}) %reduce-scatter.17.cloned.1.call-update) | async-done | bytes 294928 | tf_op jit(solution)/shard_map/reduce_scatter | solution.py:284
  967.3 141.1 %reduce-scatter.15.cloned.1.call-done = f32[24,3072]{1,0:T(8,128)} async-done(((f32[768,3072]{1,0:T(8,128)}), f32[24,3072]{1,0:T(8,128)}) %reduce-scatter.15.cloned.1.call-update) | async-done | bytes 294928 | tf_op jit(solution)/shard_map/reduce_scatter | solution.py:282
  1108.4 125.2 %reduce-scatter.11.cloned.1.call-done = f32[24,2304]{1,0:T(8,128)} async-done(((f32[768,2304]{1,0:T(8,128)}), f32[24,2304]{1,0:T(8,128)}) %reduce-scatter.11.cloned.1.call-update) | async-done | bytes 221200 | tf_op jit(solution)/shard_map/reduce_scatter | solution.py:279
  (348 shorter events, 321.8 us)
Async XLA Ops:
  7.2 66.6 %all-gather.7.cloned.1.call-start = ((), (), s32[]{:S(2)}) async-start(), calls=%async_computation.6 | async-start | bytes 3649536 | tf_op jit(solution)/shard_map/all_gather | solution.py:77
  7.9 132.4 %all-gather.11.cloned.1.call-start = ((), (), s32[]{:S(2)}) async-start(), calls=%async_computation.8 | async-start | bytes 3538944 | tf_op jit(solution)/shard_map/all_gather | solution.py:145
  57.6 22.4 %copy-start.22 = (f32[512]{0:T(512)}, f32[512]{0:T(512)S(1)}, u32[]{:S(2)}) copy-start(f32[512]{0:T(512)S(1)} %broadcast_multiply_fusion.1) | copy-start | bytes 6148
  58.5 21.5 %copy-start.24 = (f32[512]{0:T(512)}, f32[512]{0:T(512)S(1)}, u32[]{:S(2)}) copy-start(f32[512]{0:T(512)S(1)} %fusion.57) | copy-start | bytes 6148
  58.5 22.5 %copy-start.37 = (s32[1,128]{1,0:T(1,128)S(1)}, s32[1,128]{1,0:T(1,128)}, u32[]{:S(2)}) copy-start(s32[1,128]{1,0:T(1,128)} %param.20) | copy-start | bytes 1540
  58.5 22.8 %copy-start.33 = (s32[1,13]{1,0:T(1,128)S(1)}, s32[1,13]{1,0:T(1,128)}, u32[]{:S(2)}) copy-start(s32[1,13]{1,0:T(1,128)} %param.21) | copy-start | bytes 160
  81.0 123.1 %all-gather.9.cloned.1.call-start = ((), (), s32[]{:S(2)}) async-start(), calls=%async_computation.7 | async-start | bytes 3538944 | tf_op jit(solution)/shard_map/all_gather | solution.py:144
  95.6 197.8 %all-gather.13.cloned.1.call-start = ((), (), s32[]{:S(2)}) async-start(), calls=%async_computation.9 | async-start | bytes 1216512 | tf_op jit(solution)/shard_map/all_gather | solution.py:78
  96.2 228.2 %all-gather.15.cloned.1.call-start = ((), (), s32[]{:S(2)}) async-start(), calls=%async_computation.10 | async-start | bytes 4866048 | tf_op jit(solution)/shard_map/all_gather | solution.py:80
  96.8 292.9 %all-gather.17.cloned.1.call-start = ((), (), s32[]{:S(2)}) async-start(), calls=%async_computation.11 | async-start | bytes 4866048 | tf_op jit(solution)/shard_map/all_gather | solution.py:82
  97.4 546.2 %reduce-scatter.7.cloned.1.call-start = ((), (), s32[]{:S(2)}) async-start(), calls=%async_computation.12 | async-start | bytes 3538944 | tf_op jit(solution)/shard_map/reduce_scatter | solution.py:252
  144.3 59.8 %copy-start.13 = (bf16[256,12,64]{0,2,1:T(8,128)(2,1)S(1)}, bf16[256,12,64]{0,2,1:T(8,128)(2,1)}, u32[]{:S(2)}) copy-start(bf16[256,12,64]{0,2,1:T(8,128)(2,1)} %get-tuple-element.274) | copy-start | bytes 1179652
  297.4 92.3 %copy-start.5 = (bf16[1,2,256,768]{3,2,1,0:T(8,128)(2,1)S(1)}, bf16[1,2,256,768]{3,2,1,0:T(8,128)(2,1)}, u32[]{:S(2)}) copy-start(bf16[1,2,256,768]{3,2,1,0:T(8,128)(2,1)} %param.31) | copy-start | bytes 2359300
  569.7 151.7 %reduce-scatter.9.cloned.1.call-start = ((), (), s32[]{:S(2)}) async-start(), calls=%async_computation.13 | async-start | bytes 3538944 | tf_op jit(solution)/shard_map/reduce_scatter | solution.py:255
  573.7 251.8 %reduce-scatter.13.cloned.1.call-start = ((), (), s32[]{:S(2)}) async-start(), calls=%async_computation.15 | async-start | bytes 2433024 | tf_op jit(solution)/shard_map/reduce_scatter | solution.py:280
  578.3 389.1 %reduce-scatter.17.cloned.1.call-start = ((), (), s32[]{:S(2)}) async-start(), calls=%async_computation.17 | async-start | bytes 9732096 | tf_op jit(solution)/shard_map/reduce_scatter | solution.py:284
  588.5 520.0 %reduce-scatter.15.cloned.1.call-start = ((), (), s32[]{:S(2)}) async-start(), calls=%async_computation.16 | async-start | bytes 9732096 | tf_op jit(solution)/shard_map/reduce_scatter | solution.py:282
  597.0 47.6 %copy-start.19 = (f32[512,32]{0,1:T(8,128)S(1)}, f32[512,32]{0,1:T(8,128)}, u32[]{:S(2)}) copy-start(f32[512,32]{0,1:T(8,128)} %copy-done.18) | copy-start | bytes 196612
  597.1 47.6 %copy-start.21 = (f32[512,32]{0,1:T(8,128)S(1)}, f32[512,32]{0,1:T(8,128)}, u32[]{:S(2)}) copy-start(f32[512,32]{0,1:T(8,128)} %get-tuple-element.281) | copy-start | bytes 196612
  597.1 636.5 %reduce-scatter.11.cloned.1.call-start = ((), (), s32[]{:S(2)}) async-start(), calls=%async_computation.14 | async-start | bytes 7299072 | tf_op jit(solution)/shard_map/reduce_scatter | solution.py:279
  646.9 74.4 %copy-start.20 = (bf16[256,12,64]{0,2,1:T(8,128)(2,1)S(1)}, bf16[256,12,64]{0,2,1:T(8,128)(2,1)}, u32[]{:S(2)}) copy-start(bf16[256,12,64]{0,2,1:T(8,128)(2,1)} %slice.124) | copy-start | bytes 1179652
  646.9 74.4 %copy-start.23 = (f32[512]{0:T(512)S(1)}, f32[512]{0:T(512)}, u32[]{:S(2)}) copy-start(f32[512]{0:T(512)} %copy-done.22) | copy-start | bytes 6148
  647.0 74.4 %copy-start.25 = (f32[512]{0:T(512)S(1)}, f32[512]{0:T(512)}, u32[]{:S(2)}) copy-start(f32[512]{0:T(512)} %copy-done.24) | copy-start | bytes 6148
  647.0 74.4 %copy-start.27 = (f32[768]{0:T(1024)S(1)}, f32[768]{0:T(1024)}, u32[]{:S(2)}) copy-start(f32[768]{0:T(1024)} %copy-done.26) | copy-start | bytes 9220
  (29 other events, 133.1 us)
Sparse Core Ops, SparseCore 0:
  10.9 62.7 all-gather.6
  81.1 59.1 all-gather.10
  142.3 61.6 all-gather.8
  206.8 52.2 all-gather.12
  261.9 62.5 all-gather.14
  327.2 62.4 all-gather.16
  569.8 73.7 reduce-scatter.6
  647.2 74.0 reduce-scatter.8
  727.2 98.2 reduce-scatter.12
  832.8 134.4 reduce-scatter.16
  973.8 134.5 reduce-scatter.14
  1115.5 118.0 reduce-scatter.10
where the time goes:
time: 1250 us; the launch traced here: 1240 us
  waiting for transfers between devices  750 us (60%)
  matrix products  264 us (21%)
  blocking collectives  82.6 us (7%)
  local copies, waits for them, and re-layouts  80.2 us (6%)
  other arithmetic  47 us (4%)
  between operations  15 us (1%)
    reduce_scatter x1, waiting for transfers between devices, shards(): lax.psum_scatter(grad_down_w, ('leaf', 'fsdp'), scatter_dimension=0, tile...  142 us
    reduce_scatter x1, waiting for transfers between devices, shards(): lax.psum_scatter(grad_up_w, ('leaf', 'fsdp'), scatter_dimension=0, tiled=...  141 us
    reduce_scatter x1, waiting for transfers between devices, shards(): lax.psum_scatter(grad_qkv_w, ('leaf', 'fsdp'), scatter_dimension=0, tiled...  125 us
    unnamed x2, blocking collectives  82.6 us
    reduce_scatter x1, waiting for transfers between devices, shards(): lax.psum_scatter(grad_values_all[:tree_tok].astype(jnp.bfloat16), 'leaf',...  72.4 us
    all_gather x1, waiting for transfers between devices, shards(): lax.all_gather(w_down, ('leaf', 'fsdp'), axis=0, tiled=True)  57 us
    all_gather x1, waiting for transfers between devices, shards(): lax.all_gather(key_low[:rows_dev], 'leaf', axis=0, tiled=True)  53.8 us
    reduce_scatter x1, waiting for transfers between devices, shards(): lax.psum_scatter(grad_keys_all[:tree_tok].astype(jnp.bfloat16), 'leaf', s...  42.4 us
  transfers between devices with their start and end apart: 12, of which 11 were waited for; matrix products, arithmetic and copies ran while one was open for 16% of the time, Pallas kernels for 0%

commit v1 on v0

--- a/solution.py
+++ b/solution.py
@@ -8,6 +8,18 @@
 BLOCK = 16
 NEG_FILL = -1000000000.0
 EPSILON = 1e-05
+
+
+def collect(x, axis, dim):
+    ways, here, turn = (lax.axis_size(axis), lax.axis_index(axis), x.shape[dim])
+    line, have = (x, 1)
+    while have < ways:
+        line = jnp.concatenate(
+            [line, lax.ppermute(line, axis, [(d, (d - have) % ways) for d in range(ways)])],
+            axis=dim,
+        )
+        have = 2 * have
+    return jnp.roll(line, here * turn, axis=dim)
 
 
 def look_up(table, indices):
@@ -141,7 +153,7 @@
     key_low = keyed.astype(jnp.bfloat16)
     value_low = projected[:, 2 * width :].astype(jnp.bfloat16)
     tree_keys, tree_values = (
-        lax.all_gather(key_low[:rows_dev], "leaf", axis=0, tiled=True),
+        collect(key_low[:rows_dev], "leaf", 0),
         lax.all_gather(value_low[:rows_dev], "leaf", axis=0, tiled=True),
     )
     tree_tok = tree_keys.shape[0]

time: 1250 us -> 1310 us (1.048)
  waiting for transfers between devices: 750 us -> 796 us
    ppermute x0 -> x3, waiting for transfers between devices: none -> 146 us  [collect(): lax.ppermute(line, axis, [(d, (d - have) % ways) for d in range(ways)])]
    all_gather x1, waiting for transfers between devices: 53.8 us -> 0.01 us  [shards(): lax.all_gather(key_low[:rows_dev], 'leaf', axis=0, tiled=True)]
    all_gather x1, waiting for transfers between devices: 34.7 us -> 0.01 us  [shards(): lax.all_gather(value_low[:rows_dev], 'leaf', axis=0, tiled=True)]
  transfers between devices with their start and end apart: 12 -> 15, of which waited for: 11 -> 12; matrix products, arithmetic and copies ran while one was open for 16% -> 16% of each run, Pallas kernels for 0% -> 0%
where the time goes in v1:
time: 1310 us; the launch traced here: 1300 us
  waiting for transfers between devices  796 us (61%)
  matrix products  260 us (20%)
  blocking collectives  82.6 us (6%)
  local copies, waits for them, and re-layouts  80 us (6%)
  other arithmetic  56.2 us (4%)
  between operations  15.1 us (1%)
    ppermute x3, waiting for transfers between devices, collect(): lax.ppermute(line, axis, [(d, (d - have) % ways) for d in range(ways)])  146 us
    reduce_scatter x1, waiting for transfers between devices, shards(): lax.psum_scatter(grad_down_w, ('leaf', 'fsdp'), scatter_dimension=0, tile...  142 us
    reduce_scatter x1, waiting for transfers between devices, shards(): lax.psum_scatter(grad_up_w, ('leaf', 'fsdp'), scatter_dimension=0, tiled=...  141 us
    reduce_scatter x1, waiting for transfers between devices, shards(): lax.psum_scatter(grad_qkv_w, ('leaf', 'fsdp'), scatter_dimension=0, tiled...  125 us
    unnamed x2, blocking collectives  82.6 us
    reduce_scatter x1, waiting for transfers between devices, shards(): lax.psum_scatter(grad_values_all[:tree_tok].astype(jnp.bfloat16), 'leaf',...  72.5 us
    all_gather x1, waiting for transfers between devices, shards(): lax.all_gather(w_down, ('leaf', 'fsdp'), axis=0, tiled=True)  57 us
    reduce_scatter x1, waiting for transfers between devices, shards(): lax.psum_scatter(grad_keys_all[:tree_tok].astype(jnp.bfloat16), 'leaf', s...  42.4 us
  transfers between devices with their start and end apart: 15, of which 12 were waited for; matrix products, arithmetic and copies ran while one was open for 16% of the time, Pallas kernels for 0%

profile of v1, /device:TPU:0, one launch (start us, length us, event | category | flops | bytes accessed | tf_op | source)
XLA Modules:
  0.0 1297.7 jit_solution(11792042012681535285)
XLA Ops:
  12.2 42.3 %all-reduce.12 = (bf16[768]{0:T(1024)(128)(2,1)S(1)}, bf16[768]{0:T(1024)(128)(2,1)S(1)}, bf16[768]{0:T(1024)(128)(2,1)}, bf16[768]{0:T(1024)(128)(2,1)}, bf16[3072]{0:T(1024)(128)(2,1)S(1)}) all-reduce(bf16[768]{0:T(1024)(128)(2,1)S(1)} %dynamic-update-slice.1, ...), channel_id=1, replica_groups=mesh['leaf'=8,'fsdp'=4] {'leaf','fsdp'}, use_global_device_ids=true, to_apply=%add.2 | all-reduce | flops 6144 | bytes 24576
  58.5 15.2 %all-gather.7.cloned.1.call-done = bf16[768,2304]{1,0:T(8,128)(2,1)} async-done(((bf16[24,2304]{1,0:T(8,128)(2,1)}), bf16[768,2304]{1,0:T(8,128)(2,1)}) %all-gather.7.cloned.1.call-update) | async-done | bytes 3538960 | tf_op jit(solution)/shard_map/all_gather | solution.py:89
  73.7 6.2 fusion.73
  100.9 9.4 collective-permute-done
  117.3 38.8 %collective-permute-done.1 = bf16[512,768]{0,1:T(8,128)(2,1)S(1)} collective-permute-done((bf16[512,768]{0,1:T(8,128)(2,1)S(1)}, bf16[512,768]{0,1:T(8,128)(2,1)S(1)}, u32[]{:S(2)}, u32[]{:S(2)}) %collective-permute-start.1) | collective-permute-done | bytes 786464 | tf_op jit(solution)/shard_map/ppermute | solution.py:18
  170.6 97.3 %collective-permute-done.2 = bf16[1024,768]{0,1:T(8,128)(2,1)} collective-permute-done((bf16[1024,768]{0,1:T(8,128)(2,1)}, bf16[1024,768]{0,1:T(8,128)(2,1)}, u32[]{:S(2)}, u32[]{:S(2)}) %collective-permute-start.2) | collective-permute-done | bytes 1572896 | tf_op jit(solution)/shard_map/ppermute | solution.py:18
  283.1 7.9 copy.84
  296.2 67.9 %while.28 = (s32[]{:T(128)}, bf16[12,512,64]{1,2,0:T(8,128)(2,1)S(1)}, f32[12,512,1]{1,2,0:T(1,128)}, bf16[12,512,64]{2,1,0:T(8,128)(2,1)}, bf16[12,2304,64]{1,2...) while((s32[]{:T(128)}, ...), condition=%wide.region_14.15_spmd.clone, body=%wide.region_11.14_spmd.sunk.clone | while | flops 311426560 | bytes 16504921 | solution.py:177
  368.3 16.6 %all-gather.13.cloned.1.call-done = bf16[768,3072]{1,0:T(8,128)(2,1)} async-done(((bf16[24,3072]{1,0:T(8,128)(2,1)}), bf16[768,3072]{1,0:T(8,128)(2,1)}) %all-gather.13.cloned.1.call-update) | async-done | bytes 4718608 | tf_op jit(solution)/shard_map/all_gather | solution.py:92
  384.9 8.2 fusion.64
  393.1 57.0 %all-gather.15.cloned.1.call-done = bf16[3072,768]{1,0:T(8,128)(2,1)} async-done(((bf16[96,768]{1,0:T(8,128)(2,1)}), bf16[3072,768]{1,0:T(8,128)(2,1)}) %all-gather.15.cloned.1.call-update) | async-done | bytes 4718608 | tf_op jit(solution)/shard_map/all_gather | solution.py:94
  450.1 9.9 convert_reduce_fusion
  470.5 151.6 %while.29 = (s32[]{:T(128)}, f32[12,512,64]{1,2,0:T(8,128)}, f32[12,2304,64]{1,2,0:T(8,128)}, bf16[12,2304,64]{1,2,0:T(8,128)(2,1)}, bf16[12,512,64]{2,1,0:T(8,1...) while((s32[]{:T(128)}, f32[12,512,64]{1,2,0:T(8,128)}, ...), condition=%wide.region_21.22_spmd.clone, body=%wide.region_19.21_spmd.sunk.clone | while | flops 765771264 | bytes 39468144 | solution.py:250
  635.6 10.0 fusion.66
  647.1 7.2 fusion.63
  658.4 42.4 %reduce-scatter.7.cloned.1.call-done = bf16[256,768]{0,1:T(8,128)(2,1)} async-done(((bf16[2048,768]{0,1:T(8,128)(2,1)}), bf16[256,768]{0,1:T(8,128)(2,1)}) %reduce-scatter.7.cloned.1.call-update) | async-done | bytes 393232 | tf_op jit(solution)/shard_map/reduce_scatter | solution.py:264
  706.1 72.5 %reduce-scatter.9.cloned.1.call-done = bf16[256,768]{0,1:T(8,128)(2,1)} async-done(((bf16[2048,768]{0,1:T(8,128)(2,1)}), bf16[256,768]{0,1:T(8,128)(2,1)}) %reduce-scatter.9.cloned.1.call-update) | async-done | bytes 393232 | tf_op jit(solution)/shard_map/reduce_scatter | solution.py:267
  778.5 6.7 fusion.52
  787.8 9.3 add_convert_fusion
  802.6 40.2 %all-reduce.11 = (f32[768]{0:T(1024)S(1)}, f32[768]{0:T(1024)S(1)}, f32[3072]{0:T(1024)S(1)}, f32[768]{0:T(1024)S(1)}, f32[768]{0:T(1024)S(1)}) all-reduce(f32[768]{0:T(1024)S(1)} %get-tuple-element.195, f32[768]{0:T(1024)S(1)} %copy-done.35, f32[3072]{0:T(1024)S(1)} %copy-done.32, ...), channel_id=4, replica_groups=mesh['leaf'=8,'fsdp'=4] {'leaf','fsdp'}, use_global_device_ids=true, to_apply=%region_27.28.clone | all-reduce | flops 6144 | bytes 49152
  845.7 36.8 %reduce-scatter.13.cloned.1.call-done = f32[24,768]{1,0:T(8,128)} async-done(((f32[768,768]{1,0:T(8,128)}), f32[24,768]{1,0:T(8,128)}) %reduce-scatter.13.cloned.1.call-update) | async-done | bytes 73744 | tf_op jit(solution)/shard_map/reduce_scatter | solution.py:292
  882.6 141.7 %reduce-scatter.17.cloned.1.call-done = f32[96,768]{1,0:T(8,128)} async-done(((f32[3072,768]{1,0:T(8,128)}), f32[96,768]{1,0:T(8,128)}) %reduce-scatter.17.cloned.1.call-update) | async-done | bytes 294928 | tf_op jit(solution)/shard_map/reduce_scatter | solution.py:296
  1024.3 141.3 %reduce-scatter.15.cloned.1.call-done = f32[24,3072]{1,0:T(8,128)} async-done(((f32[768,3072]{1,0:T(8,128)}), f32[24,3072]{1,0:T(8,128)}) %reduce-scatter.15.cloned.1.call-update) | async-done | bytes 294928 | tf_op jit(solution)/shard_map/reduce_scatter | solution.py:294
  1165.6 125.1 %reduce-scatter.11.cloned.1.call-done = f32[24,2304]{1,0:T(8,128)} async-done(((f32[768,2304]{1,0:T(8,128)}), f32[24,2304]{1,0:T(8,128)}) %reduce-scatter.11.cloned.1.call-update) | async-done | bytes 221200 | tf_op jit(solution)/shard_map/reduce_scatter | solution.py:291
  (368 shorter events, 340.1 us)
Async XLA Ops:
  7.2 66.6 %all-gather.7.cloned.1.call-start = ((), (), s32[]{:S(2)}) async-start(), calls=%async_computation.6 | async-start | bytes 3649536 | tf_op jit(solution)/shard_map/all_gather | solution.py:89
  7.9 265.4 %all-gather.9.cloned.1.call-start = ((), (), s32[]{:S(2)}) async-start(), calls=%async_computation.7 | async-start | bytes 3538944 | tf_op jit(solution)/shard_map/all_gather | solution.py:157
  54.5 25.4 %copy-start.27 = (f32[768]{0:T(1024)}, f32[768]{0:T(1024)S(1)}, u32[]{:S(2)}) copy-start(f32[768]{0:T(1024)S(1)} %convert_element_type.105) | copy-start | bytes 9220
  80.9 210.0 %all-gather.17.cloned.1.call-start = ((), (), s32[]{:S(2)}) async-start(), calls=%async_computation.11 | async-start | bytes 3538944 | tf_op jit(solution)/shard_map/all_gather | solution.py:229
  96.5 267.5 %all-gather.11.cloned.1.call-start = ((), (), s32[]{:S(2)}) async-start(), calls=%async_computation.8 | async-start | bytes 1216512 | tf_op jit(solution)/shard_map/all_gather | solution.py:90
  97.1 287.8 %all-gather.13.cloned.1.call-start = ((), (), s32[]{:S(2)}) async-start(), calls=%async_computation.9 | async-start | bytes 4866048 | tf_op jit(solution)/shard_map/all_gather | solution.py:92
  97.7 352.4 %all-gather.15.cloned.1.call-start = ((), (), s32[]{:S(2)}) async-start(), calls=%async_computation.10 | async-start | bytes 4866048 | tf_op jit(solution)/shard_map/all_gather | solution.py:94
  97.8 12.6 collective-permute-start
  111.4 44.7 %collective-permute-start.1 = (bf16[512,768]{0,1:T(8,128)(2,1)S(1)}, bf16[512,768]{0,1:T(8,128)(2,1)S(1)}, u32[]{:S(2)}, u32[]{:S(2)}) collective-permute-start(bf16[512,768]{0,1:T(8,128)(2,1)S(1)} %pad_maximum_fusion.6), channel_id=1, source_target_pairs={{0,24},{4,28},{8,0},{12,4},{16,8},{20,12},{24,16},{28,20},{1,25},{... | collective-permute-start | bytes 2359304 | tf_op jit(solution)/shard_map/ppermute | solution.py:18
  114.5 586.2 %reduce-scatter.7.cloned.1.call-start = ((), (), s32[]{:S(2)}) async-start(), calls=%async_computation.12 | async-start | bytes 3538944 | tf_op jit(solution)/shard_map/reduce_scatter | solution.py:264
  158.7 109.2 %collective-permute-start.2 = (bf16[1024,768]{0,1:T(8,128)(2,1)}, bf16[1024,768]{0,1:T(8,128)(2,1)}, u32[]{:S(2)}, u32[]{:S(2)}) collective-permute-start(bf16[1024,768]{0,1:T(8,128)(2,1)} %pad_maximum_fusion.4), channel_id=1, source_target_pairs={{0,16},{4,20},{8,24},{12,28},{16,0},{20,4},{24,8},{28,12},{1,17},{... | collective-permute-start | bytes 4718600 | tf_op jit(solution)/shard_map/ppermute | solution.py:18
  169.3 100.3 %copy-start.9 = (bf16[512,768]{0,1:T(8,128)(2,1)S(1)}, bf16[512,768]{0,1:T(8,128)(2,1)}, u32[]{:S(2)}) copy-start(bf16[512,768]{0,1:T(8,128)(2,1)} %copy-done.8) | copy-start | bytes 2359300
  368.2 81.8 %copy-start.6 = (bf16[1,2,256,768]{3,2,1,0:T(8,128)(2,1)S(1)}, bf16[1,2,256,768]{3,2,1,0:T(8,128)(2,1)}, u32[]{:S(2)}) copy-start(bf16[1,2,256,768]{3,2,1,0:T(8,128)(2,1)} %param.31) | copy-start | bytes 2359300
  627.0 151.5 %reduce-scatter.9.cloned.1.call-start = ((), (), s32[]{:S(2)}) async-start(), calls=%async_computation.13 | async-start | bytes 3538944 | tf_op jit(solution)/shard_map/reduce_scatter | solution.py:267
  631.0 251.5 %reduce-scatter.13.cloned.1.call-start = ((), (), s32[]{:S(2)}) async-start(), calls=%async_computation.15 | async-start | bytes 2433024 | tf_op jit(solution)/shard_map/reduce_scatter | solution.py:292
  635.6 388.7 %reduce-scatter.17.cloned.1.call-start = ((), (), s32[]{:S(2)}) async-start(), calls=%async_computation.17 | async-start | bytes 9732096 | tf_op jit(solution)/shard_map/reduce_scatter | solution.py:296
  645.7 519.9 %reduce-scatter.15.cloned.1.call-start = ((), (), s32[]{:S(2)}) async-start(), calls=%async_computation.16 | async-start | bytes 9732096 | tf_op jit(solution)/shard_map/reduce_scatter | solution.py:294
  654.3 47.6 %copy-start.20 = (f32[512,32]{0,1:T(8,128)S(1)}, f32[512,32]{0,1:T(8,128)}, u32[]{:S(2)}) copy-start(f32[512,32]{0,1:T(8,128)} %copy-done.19) | copy-start | bytes 196612
  654.3 47.6 %copy-start.22 = (f32[512,32]{0,1:T(8,128)S(1)}, f32[512,32]{0,1:T(8,128)}, u32[]{:S(2)}) copy-start(f32[512,32]{0,1:T(8,128)} %get-tuple-element.283) | copy-start | bytes 196612
  654.3 636.3 %reduce-scatter.11.cloned.1.call-start = ((), (), s32[]{:S(2)}) async-start(), calls=%async_computation.14 | async-start | bytes 7299072 | tf_op jit(solution)/shard_map/reduce_scatter | solution.py:291
  701.9 76.6 %copy-start.24 = (f32[512]{0:T(512)S(1)}, f32[512]{0:T(512)}, u32[]{:S(2)}) copy-start(f32[512]{0:T(512)} %copy-done.23) | copy-start | bytes 6148
  701.9 76.6 %copy-start.26 = (f32[512]{0:T(512)S(1)}, f32[512]{0:T(512)}, u32[]{:S(2)}) copy-start(f32[512]{0:T(512)} %copy-done.25) | copy-start | bytes 6148
  701.9 76.6 %copy-start.28 = (f32[768]{0:T(1024)S(1)}, f32[768]{0:T(1024)}, u32[]{:S(2)}) copy-start(f32[768]{0:T(1024)} %copy-done.27) | copy-start | bytes 9220
  704.2 74.4 %copy-start.21 = (bf16[256,12,64]{0,2,1:T(8,128)(2,1)S(1)}, bf16[256,12,64]{0,2,1:T(8,128)(2,1)}, u32[]{:S(2)}) copy-start(bf16[256,12,64]{0,2,1:T(8,128)(2,1)} %slice.124) | copy-start | bytes 1179652
  (34 other events, 208.9 us)
Sparse Core Ops, SparseCore 0:
  10.9 62.7 all-gather.6
  81.1 75.0 all-gather.8
  158.2 105.3 all-gather.16
  266.4 52.9 all-gather.10
  322.1 62.7 all-gather.12
  387.6 62.3 all-gather.14
  627.1 73.5 reduce-scatter.6
  704.4 74.0 reduce-scatter.8
  784.4 98.1 reduce-scatter.12
  889.9 134.3 reduce-scatter.16
  1030.8 134.7 reduce-scatter.14
  1172.6 117.9 reduce-scatter.10
